TPU v7x, 32 devices: a whole 2x2x4 slice. The times are simulated.
32 devices in a mesh: dp: 4 (over z), expert: 8 (over y, x, core).
Axes of the slice: x: 2, y: 2, z: 4, core: 2. Of those that a mesh axis runs over, the one named last changes fastest.
Arguments:
- tokens: bfloat16 [8, 512, 2048], P('expert', 'dp'), may hold values from -12 to 12
- routes: int32 [8, 512, 2], P('expert', 'dp'), may hold values from 0 to 7, all different within a row; in each aligned block of 128 rows (0 to 127, 128 to 255, ..., all dimensions but the last counted through in order) at most 40 rows name the same one
- gate_code: int32 [8, 512, 2], P('expert', 'dp'), may hold values from 0 to 15
- gate_table: float32 [16], replicated, may hold values from 0.1 to 1
- w_gate: bfloat16 [8, 2048, 704], P('expert'), may hold values from -0.125 to 0.125
- w_up: bfloat16 [8, 2048, 704], P('expert'), may hold values from -0.125 to 0.125
- w_down: bfloat16 [8, 704, 2048], P('expert'), may hold values from -0.7 to 0.7
- norm_gain: float32 [2048], replicated, may hold values from 0.25 to 1.75
Outputs:
- relaid_out: bfloat16 [8, 512, 2048], P('expert', None, 'dp')
Inputs may be any that keep to these rules, and one draw needn't show every extreme that they name: Within the 128 tokens of one device (aligned blocks of positions) no expert is named by more than 40 routes, a bound that some block reaches; a token's two experts differ.
All inputs are finite; a program needn't handle non-finite values.
Results may differ from a plain program's by a relative error of at most 0.0064.
Values may be sent and summed in bfloat16 or wider, within the bound.
No kernel may reach another device: no remote copies, remote signals or barrier semaphores. Data moves between devices by JAX's collectives and lax.ppermute only.
A program may use at most 64 MiB of HBM per device.

v0:
```python
import jax
import jax.numpy as jnp
from jax import lax
from jax.sharding import PartitionSpec as P

epsilon = 1e-06


def expert_ffn(slot_block, w_gate, w_up, w_down):
    shape_in = slot_block.shape
    flat_rows = slot_block.reshape(-1, shape_in[-1])
    gate_act = jnp.dot(flat_rows, w_gate[0], preferred_element_type=jnp.float32)
    up_act = jnp.dot(flat_rows, w_up[0], preferred_element_type=jnp.float32)
    hidden = (jax.nn.silu(gate_act) * up_act).astype(jnp.bfloat16)
    result = jnp.dot(hidden, w_down[0], preferred_element_type=jnp.float32).astype(jnp.bfloat16)
    return result.reshape(shape_in)


def lookup(codes, gate_table):
    levels = gate_table.shape[0]
    match = codes[:, None] == jnp.arange(levels, dtype=jnp.int32)[None, :]
    return jnp.sum(jnp.where(match, gate_table[None, :], 0.0), axis=1)


def combine_pairs(outputs, weights):
    combined = outputs[:, 0] * weights[:, 0:1] + outputs[:, 1] * weights[:, 1:2]
    rounded = lax.optimization_barrier(combined.astype(jnp.bfloat16))
    return rounded.astype(jnp.float32)


def local(tokens, routes, gate_code, gate_table, w_gate, w_up, w_down, norm_gain):
    own_rows = tokens[0]
    tok_count, feat_width = own_rows.shape
    experts = w_gate.shape[0] * lax.axis_size("expert")
    capacity = 5 * tok_count // (2 * experts)
    route_ids = routes[0].reshape(-1)
    onehot = (route_ids[:, None] == jnp.arange(experts, dtype=jnp.int32)[None, :]).astype(jnp.int32)
    slot_pos = jnp.sum((jnp.cumsum(onehot, axis=0) - onehot) * onehot, axis=1)
    position = route_ids * capacity + slot_pos
    owner_row = (
        jnp.zeros((experts * capacity,), jnp.int32)
        .at[position]
        .set(jnp.arange(2 * tok_count, dtype=jnp.int32) // 2)
    )
    filled = jnp.zeros((experts * capacity,), jnp.bool_).at[position].set(True)
    buffer = jnp.where(filled[:, None], own_rows[owner_row], jnp.zeros((), jnp.bfloat16))
    buffer = buffer.reshape(experts, capacity, feat_width)
    level_ids = gate_code[0].reshape(-1)
    received = lax.all_to_all(buffer, "expert", split_axis=0, concat_axis=0, tiled=True)
    expert_out = expert_ffn(received, w_gate, w_up, w_down)
    returned = lax.all_to_all(expert_out, "expert", split_axis=0, concat_axis=0, tiled=True)
    outputs = (
        returned.reshape(-1, feat_width)[position]
        .astype(jnp.float32)
        .reshape(tok_count, 2, feat_width)
    )
    weights = lookup(level_ids, gate_table).reshape(tok_count, 2)
    widened = combine_pairs(outputs, weights)
    inv_rms = lax.rsqrt(jnp.mean(widened * widened, axis=1, keepdims=True) + epsilon)
    normed = (widened * inv_rms * norm_gain[None, :]).astype(jnp.bfloat16)
    relaid = lax.all_to_all(normed, "dp", split_axis=1, concat_axis=0, tiled=True)
    return relaid[None]


def solution(mesh):
    in_specs = (
        P("expert", "dp", None),
        P("expert", "dp", None),
        P("expert", "dp", None),
        P(),
        P("expert", None, None),
        P("expert", None, None),
        P("expert", None, None),
        P(),
    )
    out_specs = P("expert", None, "dp")
    return jax.shard_map(local, mesh=mesh, in_specs=in_specs, out_specs=out_specs, check_vma=False)
```

profile of v0, /device:TPU:2, one launch (start us, length us, event | category | flops | bytes accessed | tf_op | source)
XLA Modules:
  0.0 100.8 jit_solution(10024853014143610538)
XLA Ops:
  0.0 0.9 copy.24
  0.9 0.1 eq.44
  1.1 0.1 eq.40
  1.2 0.7 broadcast_multiply_fusion
  1.9 0.6 reduce-window.6
  2.5 0.2 slice_reduce_fusion.2
  2.8 0.1 copy.23
  2.9 0.1 mul.67
  3.0 0.1 fusion.25
  3.1 1.4 %scatter_custom_fusion.1 = s32[320]{0:T(512)S(1)} fusion(s32[256]{0:T(256)S(1)} %bitcast.61, s32[256]{0:T(256)S(1)} %and_select_fusion, s32[]{:T(128)} %constant.34.clone.1), kind=kCustom, calls=%fused_computation.45 | custom fusion | bytes 1284 | tf_op jit(solution)/shard_map/scatter | solution.py:43
  4.6 1.5 %scatter_custom_fusion = pred[320]{0:T(512)(128)(4,1)S(1)} fusion(s32[256]{0:T(256)S(1)} %bitcast.62, pred[256]{0:T(512)(128)(4,1)S(1)} %broadcast.79, pred[]{:T(512)} %constant.16.clone.1), kind=kCustom, calls=%fused_computation.47 | custom fusion | bytes 321 | tf_op jit(solution)/shard_map/scatter | solution.py:45
  6.1 6.1 %gather_fusion = bf16[320,2048]{1,0:T(8,128)(2,1)} fusion(bf16[128,2048]{1,0:T(8,128)(2,1)} %bitcast.53, s32[1024]{0:T(1024)S(1)} %pad_clamp_fusion.1), kind=kCustom, calls=%fused_computation | custom fusion | bytes 2622720 | tf_op jit(solution)/shard_map/gather | solution.py:46
  12.2 1.6 %broadcast_select_fusion = bf16[8,40,2048]{2,1,0:T(8,128)(2,1)S(1)} fusion(bf16[8,40,2048]{2,1,0:T(8,128)(2,1)} %bitcast.54, pred[8,40]{1,0:T(8,128)(4,1)S(1)} %broadcast_in_dim.49), kind=kLoop, calls=%fused_computation.14 | loop fusion | flops 655360 | bytes 2621760 | tf_op jit(solution)/shard_map/jit(_where)/select_n | solution.py:46
  13.9 20.7 %all_to_all.26 = bf16[8,40,2048]{2,1,0:T(8,128)(2,1)S(1)} all-to-all(bf16[8,40,2048]{2,1,0:T(8,128)(2,1)S(1)} %broadcast_select_fusion), channel_id=1, replica_groups=mesh['dp'=4,'expert'=8] {'expert'}, dimensions={0} | all-to-all | bytes 2621440 | tf_op jit(solution)/shard_map/all_to_all | solution.py:49
  34.6 1.1 %copy-done.1 = bf16[8,40,2048]{2,1,0:T(8,128)(2,1)} copy-done((bf16[8,40,2048]{2,1,0:T(8,128)(2,1)}, bf16[8,40,2048]{2,1,0:T(8,128)(2,1)S(1)}, u32[]{:S(2)}) %copy-start.1) | copy-done | bytes 1310744
  35.7 2.2 %fusion.4 = f32[320,704]{1,0:T(8,128)} fusion(bf16[320,2048]{1,0:T(8,128)(2,1)S(1)} %bitcast.59, bf16[1,2048,704]{1,2,0:T(8,128)(2,1)S(1)} %copy-done.5), kind=kOutput, calls=%fused_computation.8 | convolution fusion | flops 922746880 | bytes 5095424 | tf_op jit(solution)/shard_map/dot_general | solution.py:12
  37.9 6.1 %fusion.6 = bf16[320,2048]{1,0:T(8,128)(2,1)} fusion(bf16[1,704,2048]{2,1,0:T(8,128)(2,1)S(1)} %copy-done, bf16[320,2048]{1,0:T(8,128)(2,1)} %bitcast.60, bf16[1,2048,704]{1,2,0:T(8,128)(2,1)} %param.13, f32[320,704]{1,0:T(8,128)} %fusion.4), kind=kOutput, calls=%fused_computation.10 | convolution fusion | flops 1847500800 | bytes 9289728 | tf_op jit(solution)/shard_map/dot_general | solution.py:15
  44.0 5.7 %all-to-all-start.1 = ((bf16[8,40,2048]{2,1,0:T(8,128)(2,1)}), bf16[8,40,2048]{2,1,0:T(8,128)(2,1)}, u32[]{:S(2)}, u32[]{:S(2)}) async-start(bf16[8,40,2048]{2,1,0:T(8,128)(2,1)} %bitcast.58), calls=%async_computation.1 | async-start | bytes 2621440 | tf_op jit(solution)/shard_map/all_to_all | solution.py:51
  49.8 0.1 copy.27
  49.9 0.1 eq.48
  50.0 0.1 select_reduce_fusion
  50.1 0.1 reshape.88
  50.3 0.2 slice_reduce_fusion.1
  50.5 16.1 %all-to-all-done.1 = bf16[8,40,2048]{2,1,0:T(8,128)(2,1)} async-done(((bf16[8,40,2048]{2,1,0:T(8,128)(2,1)}), bf16[8,40,2048]{2,1,0:T(8,128)(2,1)}, u32[]{:S(2)}, u32[]{:S(2)}) %all-to-all-start.1) | async-done | bytes 1310752 | tf_op jit(solution)/shard_map/all_to_all | solution.py:51
  66.6 4.8 %gather_fusion.1 = bf16[256,2048]{1,0:T(8,128)(2,1)} fusion(bf16[320,2048]{1,0:T(8,128)(2,1)} %bitcast.11, s32[1024]{0:T(1024)S(1)} %pad_clamp_fusion), kind=kCustom, calls=%fused_computation.1 | custom fusion | bytes 2098176 | tf_op jit(solution)/shard_map/gather | solution.py:53
  71.4 3.3 %reshape.89 = f32[128,2,2048]{2,1,0:T(2,128)} reshape(bf16[256,2048]{1,0:T(8,128)(2,1)} %gather_fusion.1) | data formatting | bytes 3145728 | tf_op jit(solution)/shard_map/convert_element_type | solution.py:54
  74.8 4.4 %fusion.32 = (f32[128,1,2048]{2,1,0:T(1,128)S(1)}, f32[128,1,2048]{2,1,0:T(1,128)S(1)}) fusion(f32[128,2,2048]{2,1,0:T(2,128)} %reshape.89), kind=kLoop, calls=%fused_computation.52 | loop fusion | bytes 4194304 | tf_op jit(solution)/shard_map/slice | solution.py:26
  79.2 1.0 %fusion.20 = bf16[128,2048]{1,0:T(8,128)(2,1)S(1)} fusion(f32[128,1,2048]{2,1,0:T(1,128)S(1)} %get-tuple-element.8, f32[128,1,2048]{2,1,0:T(1,128)S(1)} %get-tuple-element.7, f32[128]{0:T(128)S(1)} %get-tuple-element.6, f32[128]{0:T(128)S(1)} %get-tuple-element.5), kind=kLoop, calls=%fused_computation.22 | loop fusion | flops 1048576 | bytes 2622464 | tf_op jit(solution)/shard_map/convert_element_type | solution.py:27
  80.2 0.2 fusion.15
  80.4 0.2 fusion.17
  80.6 19.4 %all_to_all.27 = bf16[128,4,512]{2,0,1:T(8,128)(2,1)S(1)} all-to-all(bf16[128,4,512]{2,0,1:T(8,128)(2,1)S(1)} %bitcast.56), channel_id=1, replica_groups=mesh['dp'=4,'expert'=8] {'dp'}, dimensions={1} | all-to-all | bytes 1048576 | tf_op jit(solution)/shard_map/all_to_all | solution.py:61
  100.0 0.8 copy.43
  (23 shorter events, 0.2 us)
Async XLA Ops:
  0.0 37.9 %copy-start = (bf16[1,704,2048]{2,1,0:T(8,128)(2,1)S(1)}, bf16[1,704,2048]{2,1,0:T(8,128)(2,1)}, u32[]{:S(2)}) copy-start(bf16[1,704,2048]{2,1,0:T(8,128)(2,1)} %param.14) | copy-start | bytes 8650756
  12.2 23.4 %copy-start.5 = (bf16[1,2048,704]{1,2,0:T(8,128)(2,1)S(1)}, bf16[1,2048,704]{1,2,0:T(8,128)(2,1)}, u32[]{:S(2)}) copy-start(bf16[1,2048,704]{1,2,0:T(8,128)(2,1)} %param.12) | copy-start | bytes 8650756
  34.6 1.1 %copy-start.1 = (bf16[8,40,2048]{2,1,0:T(8,128)(2,1)}, bf16[8,40,2048]{2,1,0:T(8,128)(2,1)S(1)}, u32[]{:S(2)}) copy-start(bf16[8,40,2048]{2,1,0:T(8,128)(2,1)S(1)} %all_to_all.26) | copy-start | bytes 3932164
  44.0 5.8 %copy-start.3 = (s32[1,128,2]{1,2,0:T(2,128)S(1)}, s32[1,128,2]{1,2,0:T(2,128)}, u32[]{:S(2)}) copy-start(s32[1,128,2]{1,2,0:T(2,128)} %param.10) | copy-start | bytes 3076
  44.0 6.0 %copy-start.4 = (f32[16]{0:T(128)S(1)}, f32[16]{0:T(128)}, u32[]{:S(2)}) copy-start(f32[16]{0:T(128)} %param.11) | copy-start | bytes 196
  44.0 22.5 %all-to-all-start.1 = ((bf16[8,40,2048]{2,1,0:T(8,128)(2,1)}), bf16[8,40,2048]{2,1,0:T(8,128)(2,1)}, u32[]{:S(2)}, u32[]{:S(2)}) async-start(bf16[8,40,2048]{2,1,0:T(8,128)(2,1)} %bitcast.58), calls=%async_computation.1 | async-start | bytes 2621440 | tf_op jit(solution)/shard_map/all_to_all | solution.py:51
  79.1 1.2 %copy-start.2 = (f32[2048]{0:T(1024)S(1)}, f32[2048]{0:T(1024)}, u32[]{:S(2)}) copy-start(f32[2048]{0:T(1024)} %param.15) | copy-start | bytes 24580
where the time goes:
time: 101 us
  blocking collectives  40.1 us (40%)
  local copies, waits for them, and re-layouts  25.8 us (26%)
  waiting for transfers between devices  16.1 us (16%)
  matrix products  8.36 us (8%)
  starting transfers between devices  5.75 us (6%)
  other arithmetic  4.54 us (4%)
    all_to_all x1, blocking collectives, local(): lax.all_to_all(buffer, 'expert', split_axis=0, concat_axis=0, tiled=True)  20.7 us
    all_to_all x1, blocking collectives, local(): lax.all_to_all(normed, 'dp', split_axis=1, concat_axis=0, tiled=True)  19.4 us
    all_to_all x1, waiting for transfers between devices, local(): lax.all_to_all(expert_out, 'expert', split_axis=0, concat_axis=0, tiled=T...  16.1 us
    dot_general x1, matrix products, expert_ffn(): jnp.dot(hidden, w_down[0], preferred_element_type=jnp.float32)  6.15 us
    gather x1, local copies, waits for them, and re-layouts, local(): own_rows[owner_row]  6.09 us
    all_to_all x1, starting transfers between devices, local(): lax.all_to_all(expert_out, 'expert', split_axis=0, concat_axis=0, tiled=T...  5.75 us
    gather x1, local copies, waits for them, and re-layouts, local(): returned.reshape(-1, feat_width)[position].astype(jnp.float32)  4.84 us
    slice x2, local copies, waits for them, and re-layouts, combine_pairs(): combined = outputs[:, 0] * weights[:, 0:1] + outputs[:, 1] * weights[:, 1:2]  4.55 us
  transfers between devices with their start and end apart: 1, of which 1 were waited for; matrix products, arithmetic and copies ran while one was open for 1% of the time, Pallas kernels for 0%

commit v1 on v0

--- a/solution.py
+++ b/solution.py
@@ -58,7 +58,10 @@
     widened = combine_pairs(outputs, weights)
     inv_rms = lax.rsqrt(jnp.mean(widened * widened, axis=1, keepdims=True) + epsilon)
     normed = (widened * inv_rms * norm_gain[None, :]).astype(jnp.bfloat16)
-    relaid = lax.all_to_all(normed, "dp", split_axis=1, concat_axis=0, tiled=True)
+    relaid = jnp.concatenate(
+        lax.all_to_all(jnp.stack(jnp.split(normed, lax.axis_size("dp"), axis=1)), "dp", 0, 0),
+        axis=0,
+    )
     return relaid[None]
 
 

time: 101 us -> 101 us (level)
  no operation moved by 1% of the time
where the time goes in v1:
time: 101 us
  blocking collectives  40.1 us (40%)
  local copies, waits for them, and re-layouts  25.8 us (26%)
  waiting for transfers between devices  16.1 us (16%)
  matrix products  8.36 us (8%)
  starting transfers between devices  5.75 us (6%)
  other arithmetic  4.61 us (5%)
    all_to_all x1, blocking collectives, local(): lax.all_to_all(buffer, 'expert', split_axis=0, concat_axis=0, tiled=True)  20.7 us
    all_to_all x1, blocking collectives, local(): lax.all_to_all(jnp.stack(jnp.split(normed, lax.axis_size('dp'), axis=1)),...  19.4 us
    all_to_all x1, waiting for transfers between devices, local(): lax.all_to_all(expert_out, 'expert', split_axis=0, concat_axis=0, tiled=T...  16.1 us
    dot_general x1, matrix products, expert_ffn(): jnp.dot(hidden, w_down[0], preferred_element_type=jnp.float32)  6.15 us
    gather x1, local copies, waits for them, and re-layouts, local(): own_rows[owner_row]  6.09 us
    all_to_all x1, starting transfers between devices, local(): lax.all_to_all(expert_out, 'expert', split_axis=0, concat_axis=0, tiled=T...  5.75 us
    gather x1, local copies, waits for them, and re-layouts, local(): returned.reshape(-1, feat_width)[position].astype(jnp.float32)  4.84 us
    slice x2, local copies, waits for them, and re-layouts, combine_pairs(): combined = outputs[:, 0] * weights[:, 0:1] + outputs[:, 1] * weights[:, 1:2]  4.55 us
  transfers between devices with their start and end apart: 1, of which 1 were waited for; matrix products, arithmetic and copies ran while one was open for 1% of the time, Pallas kernels for 0%

profile of v1, /device:TPU:2, one launch (start us, length us, event | category | flops | bytes accessed | tf_op | source)
XLA Modules:
  0.0 100.9 jit_solution(5468148255370982929)
XLA Ops:
  0.0 0.9 copy.21
  0.9 0.1 eq.44
  1.1 0.1 eq.40
  1.2 0.7 broadcast_multiply_fusion
  1.9 0.6 reduce-window.6
  2.5 0.2 slice_reduce_fusion.2
  2.8 0.1 copy.20
  2.9 0.1 mul.67
  3.0 0.1 fusion.25
  3.1 1.4 %scatter_custom_fusion.1 = s32[320]{0:T(512)S(1)} fusion(s32[256]{0:T(256)S(1)} %bitcast.61, s32[256]{0:T(256)S(1)} %and_select_fusion, s32[]{:T(128)} %constant.34.clone.1), kind=kCustom, calls=%fused_computation.49 | custom fusion | bytes 1284 | tf_op jit(solution)/shard_map/scatter | solution.py:43
  4.6 1.5 %scatter_custom_fusion = pred[320]{0:T(512)(128)(4,1)S(1)} fusion(s32[256]{0:T(256)S(1)} %bitcast.62, pred[256]{0:T(512)(128)(4,1)S(1)} %broadcast.79, pred[]{:T(512)} %constant.16.clone.1), kind=kCustom, calls=%fused_computation.51 | custom fusion | bytes 321 | tf_op jit(solution)/shard_map/scatter | solution.py:45
  6.1 6.1 %gather_fusion = bf16[320,2048]{1,0:T(8,128)(2,1)} fusion(bf16[128,2048]{1,0:T(8,128)(2,1)} %bitcast.55, s32[1024]{0:T(1024)S(1)} %pad_clamp_fusion.1), kind=kCustom, calls=%fused_computation | custom fusion | bytes 2622720 | tf_op jit(solution)/shard_map/gather | solution.py:46
  12.2 1.6 %broadcast_select_fusion = bf16[8,40,2048]{2,1,0:T(8,128)(2,1)S(1)} fusion(bf16[8,40,2048]{2,1,0:T(8,128)(2,1)} %bitcast.56, pred[8,40]{1,0:T(8,128)(4,1)S(1)} %broadcast_in_dim.46), kind=kLoop, calls=%fused_computation.14 | loop fusion | flops 655360 | bytes 2621760 | tf_op jit(solution)/shard_map/jit(_where)/select_n | solution.py:46
  13.9 20.7 %all_to_all.15 = bf16[8,40,2048]{2,1,0:T(8,128)(2,1)S(1)} all-to-all(bf16[8,40,2048]{2,1,0:T(8,128)(2,1)S(1)} %broadcast_select_fusion), channel_id=1, replica_groups=mesh['dp'=4,'expert'=8] {'expert'}, dimensions={0} | all-to-all | bytes 2621440 | tf_op jit(solution)/shard_map/all_to_all | solution.py:49
  34.6 1.1 %copy-done.1 = bf16[8,40,2048]{2,1,0:T(8,128)(2,1)} copy-done((bf16[8,40,2048]{2,1,0:T(8,128)(2,1)}, bf16[8,40,2048]{2,1,0:T(8,128)(2,1)S(1)}, u32[]{:S(2)}) %copy-start.1) | copy-done | bytes 1310744
  35.7 2.2 %fusion.4 = f32[320,704]{1,0:T(8,128)} fusion(bf16[320,2048]{1,0:T(8,128)(2,1)S(1)} %bitcast.59, bf16[1,2048,704]{1,2,0:T(8,128)(2,1)S(1)} %copy-done.5), kind=kOutput, calls=%fused_computation.8 | convolution fusion | flops 922746880 | bytes 5095424 | tf_op jit(solution)/shard_map/dot_general | solution.py:12
  37.9 6.1 %fusion.6 = bf16[320,2048]{1,0:T(8,128)(2,1)} fusion(bf16[1,704,2048]{2,1,0:T(8,128)(2,1)S(1)} %copy-done, bf16[320,2048]{1,0:T(8,128)(2,1)} %bitcast.60, bf16[1,2048,704]{1,2,0:T(8,128)(2,1)} %param.13, f32[320,704]{1,0:T(8,128)} %fusion.4), kind=kOutput, calls=%fused_computation.10 | convolution fusion | flops 1847500800 | bytes 9289728 | tf_op jit(solution)/shard_map/dot_general | solution.py:15
  44.0 5.7 %all-to-all-start.1 = ((bf16[8,40,2048]{2,1,0:T(8,128)(2,1)}), bf16[8,40,2048]{2,1,0:T(8,128)(2,1)}, u32[]{:S(2)}, u32[]{:S(2)}) async-start(bf16[8,40,2048]{2,1,0:T(8,128)(2,1)} %bitcast.58), calls=%async_computation.1 | async-start | bytes 2621440 | tf_op jit(solution)/shard_map/all_to_all | solution.py:51
  49.8 0.1 copy.24
  49.9 0.1 eq.48
  50.0 0.1 select_reduce_fusion
  50.1 0.1 reshape.84
  50.3 0.2 slice_reduce_fusion.1
  50.5 16.1 %all-to-all-done.1 = bf16[8,40,2048]{2,1,0:T(8,128)(2,1)} async-done(((bf16[8,40,2048]{2,1,0:T(8,128)(2,1)}), bf16[8,40,2048]{2,1,0:T(8,128)(2,1)}, u32[]{:S(2)}, u32[]{:S(2)}) %all-to-all-start.1) | async-done | bytes 1310752 | tf_op jit(solution)/shard_map/all_to_all | solution.py:51
  66.6 4.8 %gather_fusion.1 = bf16[256,2048]{1,0:T(8,128)(2,1)} fusion(bf16[320,2048]{1,0:T(8,128)(2,1)} %bitcast.11, s32[1024]{0:T(1024)S(1)} %pad_clamp_fusion), kind=kCustom, calls=%fused_computation.1 | custom fusion | bytes 2098176 | tf_op jit(solution)/shard_map/gather | solution.py:53
  71.4 3.3 %reshape.85 = f32[128,2,2048]{2,1,0:T(2,128)} reshape(bf16[256,2048]{1,0:T(8,128)(2,1)} %gather_fusion.1) | data formatting | bytes 3145728 | tf_op jit(solution)/shard_map/convert_element_type | solution.py:54
  74.8 4.4 %fusion.32 = (f32[128,1,2048]{2,1,0:T(1,128)S(1)}, f32[128,1,2048]{2,1,0:T(1,128)S(1)}) fusion(f32[128,2,2048]{2,1,0:T(2,128)} %reshape.85), kind=kLoop, calls=%fused_computation.56 | loop fusion | bytes 4194304 | tf_op jit(solution)/shard_map/slice | solution.py:26
  79.2 1.0 %fusion.20 = bf16[128,2048]{1,0:T(8,128)(2,1)S(1)} fusion(f32[128,1,2048]{2,1,0:T(1,128)S(1)} %get-tuple-element.8, f32[128,1,2048]{2,1,0:T(1,128)S(1)} %get-tuple-element.7, f32[128]{0:T(128)S(1)} %get-tuple-element.6, f32[128]{0:T(128)S(1)} %get-tuple-element.5), kind=kLoop, calls=%fused_computation.22 | loop fusion | flops 1048576 | bytes 2622464 | tf_op jit(solution)/shard_map/convert_element_type | solution.py:27
  80.2 0.2 fusion.15
  80.4 0.2 fusion.17
  80.7 19.4 %all_to_all.16 = bf16[4,128,512]{2,1,0:T(8,128)(2,1)S(1)} all-to-all(bf16[4,128,512]{2,1,0:T(8,128)(2,1)S(1)} %pad_maximum_fusion), channel_id=1, replica_groups=mesh['dp'=4,'expert'=8] {'dp'}, dimensions={0} | all-to-all | bytes 1048576 | tf_op jit(solution)/shard_map/all_to_all | solution.py:62
  100.1 0.8 copy.36
  (24 shorter events, 0.3 us)
Async XLA Ops:
  0.0 37.9 %copy-start = (bf16[1,704,2048]{2,1,0:T(8,128)(2,1)S(1)}, bf16[1,704,2048]{2,1,0:T(8,128)(2,1)}, u32[]{:S(2)}) copy-start(bf16[1,704,2048]{2,1,0:T(8,128)(2,1)} %param.14) | copy-start | bytes 8650756
  12.2 23.4 %copy-start.5 = (bf16[1,2048,704]{1,2,0:T(8,128)(2,1)S(1)}, bf16[1,2048,704]{1,2,0:T(8,128)(2,1)}, u32[]{:S(2)}) copy-start(bf16[1,2048,704]{1,2,0:T(8,128)(2,1)} %param.12) | copy-start | bytes 8650756
  34.6 1.1 %copy-start.1 = (bf16[8,40,2048]{2,1,0:T(8,128)(2,1)}, bf16[8,40,2048]{2,1,0:T(8,128)(2,1)S(1)}, u32[]{:S(2)}) copy-start(bf16[8,40,2048]{2,1,0:T(8,128)(2,1)S(1)} %all_to_all.15) | copy-start | bytes 3932164
  44.0 5.8 %copy-start.3 = (s32[1,128,2]{1,2,0:T(2,128)S(1)}, s32[1,128,2]{1,2,0:T(2,128)}, u32[]{:S(2)}) copy-start(s32[1,128,2]{1,2,0:T(2,128)} %param.10) | copy-start | bytes 3076
  44.0 6.0 %copy-start.4 = (f32[16]{0:T(128)S(1)}, f32[16]{0:T(128)}, u32[]{:S(2)}) copy-start(f32[16]{0:T(128)} %param.11) | copy-start | bytes 196
  44.0 22.5 %all-to-all-start.1 = ((bf16[8,40,2048]{2,1,0:T(8,128)(2,1)}), bf16[8,40,2048]{2,1,0:T(8,128)(2,1)}, u32[]{:S(2)}, u32[]{:S(2)}) async-start(bf16[8,40,2048]{2,1,0:T(8,128)(2,1)} %bitcast.58), calls=%async_computation.1 | async-start | bytes 2621440 | tf_op jit(solution)/shard_map/all_to_all | solution.py:51
  79.1 1.2 %copy-start.2 = (f32[2048]{0:T(1024)S(1)}, f32[2048]{0:T(1024)}, u32[]{:S(2)}) copy-start(f32[2048]{0:T(1024)} %param.15) | copy-start | bytes 24580
